TPU v7x, 32 devices: a whole 2x2x4 slice. The times are simulated.
32 devices in a mesh: tm: 2 (over y), lon: 16 (over z, x, core).
Axes of the slice: x: 2, y: 2, z: 4, core: 2. Of those that a mesh axis runs over, the one named last changes fastest.
Arguments:
- first_guess: float32 [1, 8, 128, 128], P(None, 'tm', 'lon'), may hold values from -6 to 6
- observed: float32 [1, 8, 128, 128], P(None, 'tm', 'lon'), may hold values from -6 to 6
- obs_mask: int32 [1, 8, 128, 128], P(None, 'tm', 'lon'), may hold values 0 or 1
- land_mask: int32 [128, 128], P('lon'), may hold values 0 or 1
- enc_weight: float32 [32, 27], replicated, may hold values from -1.25 to 1.25
- enc_bias: float32 [32], replicated, may hold values from -0.5 to 0.5
- dec_weight: float32 [32, 27], replicated, may hold values from -0.21875 to 0.21875
- dec_bias: float32 [1], replicated, may hold values from -1 to 1
- gate_weight: bfloat16 [192, 441], replicated, may hold values from -0.25 to 0.25
- gate_bias: float32 [192], replicated, may hold values from -1 to 1
- out_weight: float32 [48], replicated, may hold values from -0.875 to 0.875
Outputs:
- analysis: float32 [1, 8, 128, 128], P(None, 'tm', 'lon')
Inputs may be any that keep to these rules, and one draw needn't show every extreme that they name: `obs_mask`: 1 marks an observed cell on that day. `land_mask`: 1 marks a sea cell.
All inputs are finite; a program needn't handle non-finite values. No bound on the sum of `obs_mask` or of `land_mask` on one device may be relied on, other than what follows from the above.
Results may differ from a plain program's by a relative error of at most 0.00082.
Values may be sent and summed in bfloat16 or wider, within the bound.
A program may use at most 64 MiB of HBM per device.

v0:
```python
import functools

import jax
import jax.numpy as jnp
from jax import lax
from jax.experimental import pallas as pl
from jax.experimental.pallas import tpu as pltpu
from jax.sharding import PartitionSpec as P

SOLVER_ITERS = 2
HALO_DAYS = 4
SLOT = 8
EDGE = 4
MESH = pl.DeviceIdType.MESH
F32, BF16 = jnp.float32, jnp.bfloat16


def up(n, m):
    return (n + m - 1) // m * m


def iota(shape, dim):
    return lax.broadcasted_iota(jnp.int32, shape, dim)


def halves(v):
    hi = v.astype(BF16)
    return hi, (v - hi.astype(F32)).astype(BF16)


def mm(a, b):
    return jnp.dot(a, b, preferred_element_type=F32)


def mm3(ahi, alo, bhi, blo):
    return mm(ahi, bhi) + mm(ahi, blo) + mm(alo, bhi)


def column(row):
    n = row.shape[1]
    eye = iota((n, n), 0) == iota((n, n), 1)
    return jnp.sum(jnp.where(eye, jnp.broadcast_to(row, (n, n)), 0.0), axis=1, keepdims=True)


def shifts(v):
    lanes = v.shape[-1]
    lane = iota(v.shape, v.ndim - 1)
    lower = jnp.where(lane == 0, 0.0, pltpu.roll(v, 1, v.ndim - 1))
    upper = jnp.where(lane == lanes - 1, 0.0, pltpu.roll(v, lanes - 1, v.ndim - 1))
    return lower, v, upper


def tap(a, b, c, flip):
    k = 9 * a + 3 * b + c
    return 26 - k if flip else k


def build_lift(w, hi_ref, lo_ref, outs, rows_in, day_rows, offset, flip, bias=None):
    ch = w.shape[0]
    width = hi_ref.shape[1]
    q = iota((ch, width), 1)
    row = jnp.full((ch, width), -1000, jnp.int32)
    taps = [jnp.zeros((ch, width), F32) for _ in range(3)]
    for a in range(3):
        for c in range(3):
            base = a * day_rows + c * rows_in
            inside = (q >= base) & (q < base + rows_in)
            row = jnp.where(inside, q - base, row)
            for b in range(3):
                k = tap(a, b, c, flip)
                taps[b] = jnp.where(inside, w[:, k : k + 1], taps[b])
    start = jnp.zeros((ch, width), F32)
    if bias is not None:
        start = jnp.where(q == 3 * rows_in, bias, start)
    for j in range(outs):
        acc = start
        for b in range(3):
            acc = jnp.where(row == j + offset + b, taps[b], acc)
        hi, lo = halves(acc)
        hi_ref[j * ch : (j + 1) * ch, :] = hi
        lo_ref[j * ch : (j + 1) * ch, :] = lo


def build_spread(w, hi_ref, lo_ref, rows_out, first, count, flip):
    ch = w.shape[0]
    width = count * ch
    eye = (iota((27, 27), 0) == iota((27, 27), 1)).astype(BF16)
    lane = iota((rows_out, width), 1)
    col = jnp.full((rows_out, width), first, jnp.int32)
    for i in range(1, count):
        col = col + (lane >= i * ch).astype(jnp.int32)
    where_b = col - iota((rows_out, width), 0) + 1
    for part, ref in zip(halves(w), (hi_ref, lo_ref)):
        tiled = jnp.concatenate([part.astype(F32)] * count, axis=0).astype(BF16)
        flat = lax.dot_general(eye, tiled, (((1,), (1,)), ((), ())), preferred_element_type=F32)
        for a in range(3):
            for c in range(3):
                acc = jnp.zeros((rows_out, width), F32)
                for b in range(3):
                    k = tap(a, b, c, flip)
                    acc = jnp.where(where_b == b, flat[k : k + 1, :], acc)
                at = (a * 3 + c) * rows_out
                ref[at : at + rows_out, :] = acc.astype(BF16)


def kernel(
    n_t, n_l, D, L, C, S,
    x_ref, y_ref, m_ref, land_ref, ew_ref, eb_ref, dw_ref, db_ref, gw_ref, gb_ref, ow_ref,
    out_ref,
    xr, yr, mr, lr, xs_hi, xs_lo, ms_hi, ms_lo, act, pb, qb, mis_ref, g3, h3, hs, hr, cell,
    te_hi, te_lo, td_hi, td_lo, se_hi, se_lo, sd_hi, sd_lo, gwt, wst, gst,
    send, recv,
):
    N = x_ref.shape[-1]
    R = L + 2 * SLOT
    E = L + 2 * EDGE
    B = E - 4
    KX = up(3 * R + 1, 16)
    KM = up(3 * E, 16)
    KG = up(3 * E + 3, 16)
    WX, WM, WG = te_hi.shape[1], td_hi.shape[1], gwt.shape[2]
    WS = wst.shape[1]
    total = n_t * D
    W = min(total, D + 2 * HALO_DAYS)
    HALF = D // 2
    t = lax.axis_index("tm")
    l = lax.axis_index("lon")
    right = lax.rem(l + 1, n_l)
    left = lax.rem(l + n_l - 1, n_l)

    def window(tt):
        return jnp.clip(tt * D - HALO_DAYS, 0, total - W)

    o = t * D - window(t)

    if n_t > 2:
        xr[...] = jnp.zeros_like(xr)

    barrier = pltpu.get_barrier_semaphore()
    moves = [(dt, dl) for dt in (0, -1, 1) for dl in (-1, 1, 0) if (dt, dl) != (0, 0)]

    def target(dt, dl):
        return (t + dt, {-1: left, 0: l, 1: right}[dl])

    def guarded(dt, fn):
        if dt == 0:
            fn()
        else:
            pl.when((t + dt >= 0) & (t + dt < n_t))(fn)

    for dt, dl in moves:
        def greet(dt=dt, dl=dl):
            pl.semaphore_signal(barrier, inc=1, device_id=target(dt, dl), device_id_type=MESH)
        guarded(dt, greet)
    around = 2 + 3 * ((t > 0).astype(jnp.int32) + (t < n_t - 1).astype(jnp.int32))
    pl.semaphore_wait(barrier, around)

    def src_lon(dl):
        return {-1: pl.ds(0, SLOT), 0: pl.ds(0, L), 1: pl.ds(L - SLOT, SLOT)}[dl]

    def dst_lon(dl):
        return {-1: pl.ds(SLOT + L, SLOT), 0: pl.ds(SLOT, L), 1: pl.ds(0, SLOT)}[dl]

    def x_copy(it, src, base_day, base_lon, dt, dl, index, sender):
        first = {-1: 0, 0: 0, 1: D - HALO_DAYS}[dt]
        days = D if dt == 0 else HALO_DAYS
        day = sender * D + first - window(sender + dt)
        lon = src_lon(dl)
        source = src.at[pl.ds(base_day + first, days), pl.ds(base_lon + lon.start, lon.size), :]
        return pltpu.make_async_remote_copy(
            src_ref=source,
            dst_ref=xr.at[it, pl.ds(day, days), dst_lon(dl), :],
            send_sem=send.at[index], recv_sem=recv.at[index],
            device_id=target(dt, dl), device_id_type=MESH,
        )

    def plain_copy(src, dst, dl, index):
        return pltpu.make_async_remote_copy(
            src_ref=src, dst_ref=dst, send_sem=send.at[index], recv_sem=recv.at[index],
            device_id=target(0, dl), device_id_type=MESH,
        )

    def x_start(it, src, base_day, base_lon, slot0):
        for i, (dt, dl) in enumerate(moves):
            def go(i=i, dt=dt, dl=dl):
                x_copy(it, src, base_day, base_lon, dt, dl, slot0 + i, t).start()
            guarded(dt, go)

    def x_wait(it, src, base_day, base_lon, slot0):
        for i, (dt, dl) in enumerate(moves):
            def got(i=i, dt=dt, dl=dl):
                x_copy(it, src, base_day, base_lon, dt, dl, slot0 + i, t - dt).wait_recv()
            def sent(i=i, dt=dt, dl=dl):
                x_copy(it, src, base_day, base_lon, dt, dl, slot0 + i, t).wait_send()
            guarded(-dt, got)
            guarded(dt, sent)

    x_start(0, x_ref, 0, 0, 0)
    others = []
    for i, dl in enumerate((-1, 1)):
        others.append(plain_copy(y_ref.at[:, src_lon(dl), :], yr.at[:, dst_lon(dl), :], dl, 8 + i))
        others.append(plain_copy(m_ref.at[:, src_lon(dl), :], mr.at[:, dst_lon(dl), :], dl, 10 + i))
        others.append(plain_copy(land_ref.at[src_lon(dl), :], lr.at[dst_lon(dl), :], dl, 12 + i))
    for copy in others:
        copy.start()

    own = pl.ds(SLOT, L)
    xr[0, pl.ds(o, D), own, :] = x_ref[...]
    yr[:, own, :] = y_ref[...]
    mr[:, own, :] = m_ref[...]
    lr[own, :] = land_ref[...]
    for ref in (ms_hi, ms_lo, pb, qb, g3):
        ref[...] = jnp.zeros_like(ref)
    for ref in (xs_hi, xs_lo):
        ref[0 : KX, :] = jnp.zeros((KX, N), BF16)
        ref[(W + 1) * KX :, :] = jnp.zeros((ref.shape[0] - (W + 1) * KX, N), BF16)
    tail = (iota((KX - 3 * R, N), 0) == 0).astype(F32)
    xs_hi[0 : KX, :] = jnp.concatenate([jnp.zeros((3 * R, N), F32), tail], axis=0).astype(BF16)
    h3[D * (L + 2) * 3 * S :, :] = jnp.zeros((h3.shape[0] - D * (L + 2) * 3 * S, N), BF16)
    for d in range(D):
        at = (d * (L + 2) + L + 1) * 3 * S
        h3[at : at + 3 * S, :] = jnp.zeros((3 * S, N), BF16)

    ew, dw = ew_ref[...], dw_ref[...]
    build_lift(ew, te_hi, te_lo, E, R, KX, SLOT - EDGE - 1, False, column(eb_ref[...]))
    build_spread(dw, sd_hi, sd_lo, E, 0, E, False)
    build_lift(dw, td_hi, td_lo, B, E, KM, 1, True)
    build_spread(ew, se_hi, se_lo, E, 2, B, True)

    wide = gw_ref[...].astype(F32)
    gate_rows = iota((4 * S, 1), 0)
    scale = jnp.where((gate_rows >= 2 * S) & (gate_rows < 3 * S), 1.0, 0.5)
    wide = wide * scale
    gbias = column(gb_ref[...]) * scale
    b_hi, b_rest = gbias.astype(BF16), None
    b_rest = gbias - b_hi.astype(F32)
    b_mid = b_rest.astype(BF16).astype(F32)
    b_low = b_rest - b_mid
    ins = S + 1
    q = iota((4 * S, WG), 1)
    start = jnp.where(q == 3 * E, b_hi.astype(F32), 0.0)
    start = jnp.where(q == 3 * E + 1, b_mid, start)
    start = jnp.where(q == 3 * E + 2, b_low, start)
    row = jnp.full((4 * S, WG), -1000, jnp.int32)
    taps = [jnp.zeros((4 * S, WG), F32) for _ in range(3)]
    for c in range(3):
        inside = (q >= c * E) & (q < (c + 1) * E)
        row = jnp.where(inside, q - c * E, row)
        for b in range(3):
            k = (3 * b + c) * ins
            taps[b] = jnp.where(inside, wide[:, k : k + 1], taps[b])
    for j in range(L):
        acc = start
        for b in range(3):
            acc = jnp.where(row == j + EDGE - 1 + b, taps[b], acc)
        gwt[j] = acc.astype(BF16)

    oweight = jnp.broadcast_to(column(ow_ref[...]), (S, 2 * N))
    dbias = db_ref[0]

    def finish(parts):
        lower, mid, upper = parts
        lane = iota(lower.shape, 1)
        return (
            jnp.where(lane == 0, 0.0, pltpu.roll(lower, 1, 1))
            + mid
            + jnp.where(lane == N - 1, 0.0, pltpu.roll(upper, N - 1, 1))
        )

    def gather_taps(ref, d):
        parts = []
        for c in range(3):
            parts.append(
                ref[d, c * E : (c + 1) * E, :]
                + ref[d + 1, (3 + c) * E : (4 + c) * E, :]
                + ref[d + 2, (6 + c) * E : (7 + c) * E, :]
            )
        return finish(parts)

    def pair(ref, d, rows, width):
        return jnp.concatenate(
            [ref[pl.ds(pl.multiple_of((d + i) * rows, 16), width), :] for i in range(2)], axis=1
        )

    def span(radius):
        n = min(W, D + 2 * radius)
        return jnp.clip(o - radius, 0, W - n), n

    edge_rows = pl.ds(SLOT - EDGE, E)

    def gradient(it):
        def stage_x(d, carry):
            f = xr[it, d]
            low, mid, high = shifts(f)
            v = jnp.concatenate([low, mid, high, tail], axis=0)
            hi, lo = halves(v)
            at = pl.ds(pl.multiple_of((d + 1) * KX, 16), KX)
            xs_hi[at, :] = hi
            xs_lo[at, :] = lo
            return carry

        lax.fori_loop(0, W, stage_x, 0)

        s3, n3 = span(3)

        def encode(p, carry):
            d = s3 + 2 * p
            enc = mm3(te_hi[...], te_lo[...], pair(xs_hi, d, KX, WX), pair(xs_lo, d, KX, WX))
            hi, lo = halves(jnp.maximum(enc, 0.0))
            out = mm3(sd_hi[...], sd_lo[...], hi, lo)
            for i in range(2):
                act[d + i] = hi[2 * C : (2 + B) * C, i * N : (i + 1) * N]
                pb[d + i + 1] = out[:, i * N : (i + 1) * N]
            return carry

        lax.fori_loop(0, n3 // 2, encode, 0)

        s2, n2 = span(2)
        sea = lr[edge_rows, :].astype(F32)

        def misfit(i, carry):
            d = s2 + i
            rebuilt = gather_taps(pb, d) + dbias
            mis = sea * (xr[it, d, edge_rows, :] - rebuilt)
            mis_ref[d] = mis
            parts = list(shifts(mis))
            if KM > 3 * E:
                parts.append(jnp.zeros((KM - 3 * E, N), F32))
            hi, lo = halves(jnp.concatenate(parts, axis=0))
            at = pl.ds(pl.multiple_of((d + 1) * KM, 16), KM)
            ms_hi[at, :] = hi
            ms_lo[at, :] = lo
            return carry

        lax.fori_loop(0, n2, misfit, 0)

        s1, n1 = span(1)

        def backward(p, carry):
            d = s1 + 2 * p
            lifted = mm3(td_hi[...], td_lo[...], pair(ms_hi, d, KM, WM), pair(ms_lo, d, KM, WM))
            on = jnp.concatenate([act[d], act[d + 1]], axis=1).astype(F32)
            hi, lo = halves(jnp.where(on > 0.0, lifted, 0.0))
            out = mm3(se_hi[...], se_lo[...], hi, lo)
            for i in range(2):
                qb[d + i + 1] = out[:, i * N : (i + 1) * N]
            return carry

        lax.fori_loop(0, n1 // 2, backward, 0)

        ones = (iota((KG - 3 * E, N), 0) < 3).astype(F32)

        def collect(i, carry):
            d = o + i
            back = gather_taps(qb, d)
            seen = mr[i, edge_rows, :].astype(F32)
            grad = (
                2.0 * seen * (xr[it, d, edge_rows, :] - yr[i, edge_rows, :]) + mis_ref[d] - back
            )
            v = jnp.concatenate(list(shifts(grad)) + [ones], axis=0)
            g3[pl.ds(pl.multiple_of(i * KG, 16), KG), :] = v.astype(BF16)
            return carry

        lax.fori_loop(0, D, collect, 0)

    def sig(v):
        return 0.5 * jnp.tanh(v) + 0.5

    def h_copies():
        return [
            plain_copy(hs.at[0], hr.at[1], -1, 22),
            plain_copy(hs.at[1], hr.at[0], 1, 23),
        ]

    def put_h3(d, lon, h):
        v = jnp.concatenate(list(shifts(h)), axis=0).astype(BF16)
        h3[pl.ds(pl.multiple_of((d * (L + 2) + lon) * 3 * S, 16), 3 * S), :] = v

    for copy in others:
        copy.wait()
    x_wait(0, x_ref, 0, 0, 0)
    gradient(0)

    def first_gates(j, carry):
        for p in range(HALF):
            rhs = pair(g3, 2 * p, KG, WG)
            up_ = mm(gwt[j, 0:S, :], rhs)
            rest = mm(gwt[j, 2 * S : 4 * S, :], rhs)
            state = sig(up_) * jnp.tanh(rest[0:S])
            hidden = sig(rest[S : 2 * S]) * jnp.tanh(state)
            cell[j, p] = state
            step = jnp.sum(oweight * hidden, axis=0, keepdims=True)
            for i in range(2):
                d = 2 * p + i
                h = hidden[:, i * N : (i + 1) * N]
                put_h3(d, j + 1, h)
                at = pl.ds(SLOT + j, 1)
                xr[1, o + d, at, :] = xr[0, o + d, at, :] - step[:, i * N : (i + 1) * N]
                for side, lon in ((0, 0), (1, L - 1)):
                    @pl.when(j == lon)
                    def _(side=side, d=d, h=h):
                        hs[side, d] = h.astype(BF16)
        return carry

    lax.fori_loop(0, L, first_gates, 0)
    x_start(1, xr.at[1], o, SLOT, 14)
    for copy in h_copies():
        copy.start()

    for base in range(0, WS, 128):
        src = iota((9 * ins, 128), 0)
        lane = iota((9 * ins, 128), 1) + base
        want = lane + 1
        for i in range(1, 9):
            want = want + (lane >= i * S).astype(jnp.int32)
        pick = ((src == want) & (lane < 9 * S)).astype(F32).astype(BF16)
        wst[:, base : base + 128] = mm(wide.astype(BF16), pick).astype(BF16)

    def state_part(j):
        for p in range(HALF):
            rhs = jnp.concatenate(
                [
                    h3[pl.ds(pl.multiple_of(((2 * p + i) * (L + 2) + j) * 3 * S, 16), WS), :]
                    for i in range(2)
                ],
                axis=1,
            )
            gst[j, p] = mm(wst[...], rhs)

    def inner(j, carry):
        state_part(j)
        return carry

    lax.fori_loop(1, L - 1, inner, 0)
    for copy in h_copies():
        copy.wait()
    for d in range(D):
        put_h3(d, 0, hr[0, d].astype(F32))
        put_h3(d, L + 1, hr[1, d].astype(F32))
    state_part(0)
    state_part(L - 1)
    x_wait(1, xr.at[1], o, SLOT, 14)
    gradient(1)

    def last_gates(j, carry):
        for p in range(HALF):
            rhs = pair(g3, 2 * p, KG, WG)
            sums = gst[j, p] + mm(gwt[j], rhs)
            state = sig(sums[S : 2 * S]) * cell[j, p] + sig(sums[0:S]) * jnp.tanh(
                sums[2 * S : 3 * S]
            )
            hidden = sig(sums[3 * S :]) * jnp.tanh(state)
            step = jnp.sum(oweight * hidden, axis=0, keepdims=True)
            for i in range(2):
                d = 2 * p + i
                out_ref[d, pl.ds(j, 1), :] = (
                    xr[1, o + d, pl.ds(SLOT + j, 1), :] - step[:, i * N : (i + 1) * N]
                )
        return carry

    lax.fori_loop(0, L, last_gates, 0)


def body(n_t, n_l, x, y, m, land, ew, eb, dw, db, gw, gb, ow):
    D, L, N = x.shape[1:]
    C = eb.shape[0]
    S = ow.shape[0]
    R, E = L + 2 * SLOT, L + 2 * EDGE
    B = E - 4
    W = min(n_t * D, D + 2 * HALO_DAYS)
    KX, KM, KG = up(3 * R + 1, 16), up(3 * E, 16), up(3 * E + 3, 16)
    WX, WM, WG, WS = up(3 * KX, 128), up(3 * KM, 128), up(KG, 128), up(9 * S, 128)
    G = 4 * S
    vm = pltpu.VMEM
    scratch = [
        vm((2, W, R, N), F32), vm((D, R, N), F32), vm((D, R, N), jnp.int32), vm((R, N), jnp.int32),
        vm(((W + 2) * KX + WX - 3 * KX, N), BF16), vm(((W + 2) * KX + WX - 3 * KX, N), BF16),
        vm(((W + 2) * KM + WM - 3 * KM, N), BF16), vm(((W + 2) * KM + WM - 3 * KM, N), BF16),
        vm((W, B * C, N), BF16), vm((W + 2, 9 * E, N), F32), vm((W + 2, 9 * E, N), F32),
        vm((W, E, N), F32), vm((D * KG + WG - KG, N), BF16),
        vm((D * (L + 2) * 3 * S + WS - 9 * S, N), BF16),
        vm((2, D, S, N), BF16), vm((2, D, S, N), BF16), vm((L, D // 2, S, 2 * N), F32),
        vm((E * C, WX), BF16), vm((E * C, WX), BF16), vm((B * C, WM), BF16), vm((B * C, WM), BF16),
        vm((9 * E, B * C), BF16), vm((9 * E, B * C), BF16),
        vm((9 * E, E * C), BF16), vm((9 * E, E * C), BF16),
        vm((L, G, WG), BF16), vm((G, WS), BF16), vm((L, D // 2, G, 2 * N), F32),
        pltpu.SemaphoreType.DMA((24,)), pltpu.SemaphoreType.DMA((24,)),
    ]
    v = pl.BlockSpec(memory_space=pltpu.VMEM)
    specs = [v] * 7 + [pl.BlockSpec(memory_space=pltpu.SMEM)] + [v] * 3
    out = pl.pallas_call(
        functools.partial(kernel, n_t, n_l, D, L, C, S),
        out_shape=jax.ShapeDtypeStruct((D, L, N), F32),
        in_specs=specs,
        out_specs=v,
        scratch_shapes=scratch,
        compiler_params=pltpu.CompilerParams(
            collective_id=0, has_side_effects=True, vmem_limit_bytes=48 << 20
        ),
        name="solver",
    )(x[0], y[0], m[0], land, ew, eb[None], dw, db, gw, gb[None], ow[None])
    return out[None]


def solution(mesh):
    tile = P(None, "tm", "lon", None)
    run = functools.partial(body, mesh.shape["tm"], mesh.shape["lon"])
    return jax.shard_map(
        run, mesh=mesh, in_specs=(tile, tile, tile, P("lon", None)) + (P(),) * 7,
        out_specs=tile, check_vma=False,
    )
```

profile of v0, /device:TPU:0, one launch (start us, length us, event | category | flops | bytes accessed | tf_op | source)
XLA Modules:
  0.0 45.4 jit_solution(864247090530063163)
XLA Ops:
  0.7 0.0 copy-start.6
  0.7 0.0 copy-start.9
  0.7 0.0 copy-start.7
  0.7 0.0 copy-start.8
  0.7 0.6 %copy-done.6 = s32[8,128]{1,0:T(8,128)S(1)} copy-done((s32[8,128]{1,0:T(8,128)S(1)}, s32[8,128]{1,0:T(8,128)}, u32[]{:S(2)}) %copy-start.6) | copy-done | bytes 4120
  1.3 0.0 copy-done.9
  1.3 0.0 copy-done.7
  1.4 0.0 copy-done.8
  1.4 0.0 copy-start
  1.4 0.9 %copy-done = bf16[192,441]{1,0:T(8,128)(2,1)S(1)} copy-done((bf16[192,441]{1,0:T(8,128)(2,1)S(1)}, bf16[192,441]{1,0:T(8,128)(2,1)}, u32[]{:S(2)}) %copy-start) | copy-done | bytes 169368
  2.3 0.0 copy-start.1
  2.3 0.7 %copy-done.1 = f32[1,4,8,128]{3,2,1,0:T(8,128)S(1)} copy-done((f32[1,4,8,128]{3,2,1,0:T(8,128)S(1)}, f32[1,4,8,128]{3,2,1,0:T(8,128)}, u32[]{:S(2)}) %copy-start.1) | copy-done | bytes 16408
  3.0 0.0 copy-start.2
  3.0 0.7 %copy-done.2 = f32[1,4,8,128]{3,2,1,0:T(8,128)S(1)} copy-done((f32[1,4,8,128]{3,2,1,0:T(8,128)S(1)}, f32[1,4,8,128]{3,2,1,0:T(8,128)}, u32[]{:S(2)}) %copy-start.2) | copy-done | bytes 16408
  3.7 0.0 copy-start.3
  3.7 0.7 %copy-done.3 = s32[1,4,8,128]{3,2,1,0:T(8,128)S(1)} copy-done((s32[1,4,8,128]{3,2,1,0:T(8,128)S(1)}, s32[1,4,8,128]{3,2,1,0:T(8,128)}, u32[]{:S(2)}) %copy-start.3) | copy-done | bytes 16408
  4.4 0.0 copy-start.4
  4.5 0.7 %copy-done.4 = f32[32,27]{1,0:T(8,128)S(1)} copy-done((f32[32,27]{1,0:T(8,128)S(1)}, f32[32,27]{1,0:T(8,128)}, u32[]{:S(2)}) %copy-start.4) | copy-done | bytes 3480
  5.2 0.0 copy-start.5
  5.2 0.7 %copy-done.5 = f32[32,27]{1,0:T(8,128)S(1)} copy-done((f32[32,27]{1,0:T(8,128)S(1)}, f32[32,27]{1,0:T(8,128)}, u32[]{:S(2)}) %copy-start.5) | copy-done | bytes 3480
  5.9 38.9 %solver.1 = f32[4,8,128]{2,1,0:T(8,128)S(1)} custom-call(f32[4,8,128]{2,1,0:T(8,128)S(1)} %bitcast.8, f32[4,8,128]{2,1,0:T(8,128)S(1)} %bitcast.9, s32[4,8,128]{2,1,0:T(8,128)S(1)} %bitcast.10, s32[8,128]{1,0:T(8,128)S(1)} %copy-done.6, f32[32,27]{1,0:T(8,128)S(1)} %copy-done.4, f32[1,32]{1,0:T(1,128)S(1)} %bitcast.12, f32[32,27]{1,0:T(8,128)S(1)} %copy-done.5, ...), custom_call_target="tpu_custom_call" | custom-call | tf_op jit(solution)/shard_map/solver/pallas_call | solution.py:491
  44.8 0.6 %copy.14 = f32[1,4,8,128]{3,2,1,0:T(8,128)} copy(f32[1,4,8,128]{3,2,1,0:T(8,128)S(1)} %bitcast.7) | data formatting | bytes 32768
Async XLA Ops:
  0.7 0.7 %copy-start.6 = (s32[8,128]{1,0:T(8,128)S(1)}, s32[8,128]{1,0:T(8,128)}, u32[]{:S(2)}) copy-start(s32[8,128]{1,0:T(8,128)} %land_ref.1) | copy-start | bytes 12292
  0.7 0.7 %copy-start.9 = (f32[48]{0:T(128)S(1)}, f32[48]{0:T(128)}, u32[]{:S(2)}) copy-start(f32[48]{0:T(128)} %param.21) | copy-start | bytes 580
  0.7 0.7 %copy-start.7 = (f32[192]{0:T(256)S(1)}, f32[192]{0:T(256)}, u32[]{:S(2)}) copy-start(f32[192]{0:T(256)} %param.20) | copy-start | bytes 2308
  0.7 0.7 %copy-start.8 = (f32[32]{0:T(128)S(1)}, f32[32]{0:T(128)}, u32[]{:S(2)}) copy-start(f32[32]{0:T(128)} %param.16) | copy-start | bytes 388
  1.4 0.9 %copy-start = (bf16[192,441]{1,0:T(8,128)(2,1)S(1)}, bf16[192,441]{1,0:T(8,128)(2,1)}, u32[]{:S(2)}) copy-start(bf16[192,441]{1,0:T(8,128)(2,1)} %gw_ref.1) | copy-start | bytes 508036
  2.3 0.7 %copy-start.1 = (f32[1,4,8,128]{3,2,1,0:T(8,128)S(1)}, f32[1,4,8,128]{3,2,1,0:T(8,128)}, u32[]{:S(2)}) copy-start(f32[1,4,8,128]{3,2,1,0:T(8,128)} %param.11) | copy-start | bytes 49156
  3.0 0.7 %copy-start.2 = (f32[1,4,8,128]{3,2,1,0:T(8,128)S(1)}, f32[1,4,8,128]{3,2,1,0:T(8,128)}, u32[]{:S(2)}) copy-start(f32[1,4,8,128]{3,2,1,0:T(8,128)} %param.12) | copy-start | bytes 49156
  3.7 0.7 %copy-start.3 = (s32[1,4,8,128]{3,2,1,0:T(8,128)S(1)}, s32[1,4,8,128]{3,2,1,0:T(8,128)}, u32[]{:S(2)}) copy-start(s32[1,4,8,128]{3,2,1,0:T(8,128)} %param.13) | copy-start | bytes 49156
  4.4 0.7 %copy-start.4 = (f32[32,27]{1,0:T(8,128)S(1)}, f32[32,27]{1,0:T(8,128)}, u32[]{:S(2)}) copy-start(f32[32,27]{1,0:T(8,128)} %ew_ref.1) | copy-start | bytes 10372
  5.2 0.7 %copy-start.5 = (f32[32,27]{1,0:T(8,128)S(1)}, f32[32,27]{1,0:T(8,128)}, u32[]{:S(2)}) copy-start(f32[32,27]{1,0:T(8,128)} %dw_ref.1) | copy-start | bytes 10372
where the time goes:
time: 46.1 us; the launch traced here: 45.4 us
  Pallas kernels  38.9 us (84%)
  local copies, waits for them, and re-layouts  5.8 us (13%)
  between operations  0.7 us (2%)
    pallas_call x1, Pallas kernels, body(): pl.pallas_call(functools.partial(kernel, n_t, n_l, D, L, C, S), out_shape...  38.9 us
    unnamed x21, local copies, waits for them, and re-layouts  5.8 us

commit v1 on v0

--- a/solution.py
+++ b/solution.py
@@ -78,10 +78,11 @@
             acc = jnp.where(row == j + offset + b, taps[b], acc)
         hi, lo = halves(acc)
         hi_ref[j * ch : (j + 1) * ch, :] = hi
-        lo_ref[j * ch : (j + 1) * ch, :] = lo
-
-
-def build_spread(w, hi_ref, lo_ref, rows_out, first, count, flip):
+        if lo_ref is not None:
+            lo_ref[j * ch : (j + 1) * ch, :] = lo
+
+
+def build_spread(w, out_ref, rows_out, first, count, flip):
     ch = w.shape[0]
     width = count * ch
     eye = (iota((27, 27), 0) == iota((27, 27), 1)).astype(BF16)
@@ -90,26 +91,34 @@
     for i in range(1, count):
         col = col + (lane >= i * ch).astype(jnp.int32)
     where_b = col - iota((rows_out, width), 0) + 1
-    for part, ref in zip(halves(w), (hi_ref, lo_ref)):
-        tiled = jnp.concatenate([part.astype(F32)] * count, axis=0).astype(BF16)
-        flat = lax.dot_general(eye, tiled, (((1,), (1,)), ((), ())), preferred_element_type=F32)
-        for a in range(3):
-            for c in range(3):
-                acc = jnp.zeros((rows_out, width), F32)
-                for b in range(3):
-                    k = tap(a, b, c, flip)
-                    acc = jnp.where(where_b == b, flat[k : k + 1, :], acc)
-                at = (a * 3 + c) * rows_out
-                ref[at : at + rows_out, :] = acc.astype(BF16)
+    tiled = jnp.concatenate([w] * count, axis=0).astype(BF16)
+    flat = lax.dot_general(eye, tiled, (((1,), (1,)), ((), ())), preferred_element_type=F32)
+    for a in range(3):
+        for c in range(3):
+            acc = jnp.zeros((rows_out, width), F32)
+            for b in range(3):
+                k = tap(a, b, c, flip)
+                acc = jnp.where(where_b == b, flat[k : k + 1, :], acc)
+            at = (a * 3 + c) * rows_out
+            out_ref[at : at + rows_out, :] = acc.astype(BF16)
 
 
 def kernel(
     n_t, n_l, D, L, C, S,
-    x_ref, y_ref, m_ref, land_ref, ew_ref, eb_ref, dw_ref, db_ref, gw_ref, gb_ref, ow_ref,
-    out_ref,
-    xr, yr, mr, lr, xs_hi, xs_lo, ms_hi, ms_lo, act, pb, qb, mis_ref, g3, h3, hs, hr, cell,
-    te_hi, te_lo, td_hi, td_lo, se_hi, se_lo, sd_hi, sd_lo, gwt, wst, gst,
-    send, recv,
+    x_ref, y_ref, m_ref, land_ref, *rest,
+):
+    weights, out_ref, filled = rest[:7], rest[7], rest[8:15]
+    kernel_body(
+        n_t, n_l, D, L, C, S, x_ref, y_ref, m_ref, land_ref, weights, filled, out_ref, *rest[15:]
+    )
+
+
+def kernel_body(
+    n_t, n_l, D, L, C, S,
+    x_ref, y_ref, m_ref, land_ref, weights, filled, out_ref,
+    xr, yr, mr, lr, xs_hi, xs_lo, ms, act, pb, qb, mis_ref, g3, h3, hs, hr, cell,
+    te_hi, te_lo, td, se, sd, gwt, wst, gst,
+    send, recv, local,
 ):
     N = x_ref.shape[-1]
     R = L + 2 * SLOT
@@ -118,7 +127,7 @@
     KX = up(3 * R + 1, 16)
     KM = up(3 * E, 16)
     KG = up(3 * E + 3, 16)
-    WX, WM, WG = te_hi.shape[1], td_hi.shape[1], gwt.shape[2]
+    WX, WM, WG = te_hi.shape[1], td.shape[1], gwt.shape[2]
     WS = wst.shape[1]
     total = n_t * D
     W = min(total, D + 2 * HALO_DAYS)
@@ -132,6 +141,14 @@
         return jnp.clip(tt * D - HALO_DAYS, 0, total - W)
 
     o = t * D - window(t)
+
+    own = pl.ds(SLOT, L)
+    ew_ref, eb_ref, dw_ref, db_ref, gw_ref, gb_ref, ow_ref = filled
+    fetches = [
+        pltpu.make_async_copy(a, b, local.at[i]) for i, (a, b) in enumerate(zip(weights, filled))
+    ]
+    for copy in fetches:
+        copy.start()
 
     if n_t > 2:
         xr[...] = jnp.zeros_like(xr)
@@ -204,12 +221,15 @@
     for copy in others:
         copy.start()
 
-    own = pl.ds(SLOT, L)
-    xr[0, pl.ds(o, D), own, :] = x_ref[...]
-    yr[:, own, :] = y_ref[...]
-    mr[:, own, :] = m_ref[...]
-    lr[own, :] = land_ref[...]
-    for ref in (ms_hi, ms_lo, pb, qb, g3):
+    tiles = [
+        pltpu.make_async_copy(x_ref, xr.at[0, pl.ds(o, D), own, :], local.at[7]),
+        pltpu.make_async_copy(y_ref, yr.at[:, own, :], local.at[8]),
+        pltpu.make_async_copy(m_ref, mr.at[:, own, :], local.at[9]),
+        pltpu.make_async_copy(land_ref, lr.at[own, :], local.at[10]),
+    ]
+    for copy in tiles:
+        copy.start()
+    for ref in (ms, pb, qb, g3):
         ref[...] = jnp.zeros_like(ref)
     for ref in (xs_hi, xs_lo):
         ref[0 : KX, :] = jnp.zeros((KX, N), BF16)
@@ -221,11 +241,13 @@
         at = (d * (L + 2) + L + 1) * 3 * S
         h3[at : at + 3 * S, :] = jnp.zeros((3 * S, N), BF16)
 
+    for copy in fetches:
+        copy.wait()
     ew, dw = ew_ref[...], dw_ref[...]
     build_lift(ew, te_hi, te_lo, E, R, KX, SLOT - EDGE - 1, False, column(eb_ref[...]))
-    build_spread(dw, sd_hi, sd_lo, E, 0, E, False)
-    build_lift(dw, td_hi, td_lo, B, E, KM, 1, True)
-    build_spread(ew, se_hi, se_lo, E, 2, B, True)
+    build_spread(dw, sd, E, 0, E, False)
+    build_lift(dw, td, None, B, E, KM, 1, True)
+    build_spread(ew, se, E, 2, B, True)
 
     wide = gw_ref[...].astype(F32)
     gate_rows = iota((4 * S, 1), 0)
@@ -255,6 +277,15 @@
             acc = jnp.where(row == j + EDGE - 1 + b, taps[b], acc)
         gwt[j] = acc.astype(BF16)
 
+    for base in range(0, WS, 128):
+        src = iota((9 * ins, 128), 0)
+        lane = iota((9 * ins, 128), 1) + base
+        want = lane + 1
+        for i in range(1, 9):
+            want = want + (lane >= i * S).astype(jnp.int32)
+        pick = ((src == want) & (lane < 9 * S)).astype(F32).astype(BF16)
+        wst[:, base : base + 128] = mm(wide.astype(BF16), pick).astype(BF16)
+
     oweight = jnp.broadcast_to(column(ow_ref[...]), (S, 2 * N))
     dbias = db_ref[0]
 
@@ -299,21 +330,23 @@
             xs_lo[at, :] = lo
             return carry
 
-        lax.fori_loop(0, W, stage_x, 0)
+        for i in range(W):
+            stage_x(i, 0)
 
         s3, n3 = span(3)
 
         def encode(p, carry):
             d = s3 + 2 * p
             enc = mm3(te_hi[...], te_lo[...], pair(xs_hi, d, KX, WX), pair(xs_lo, d, KX, WX))
-            hi, lo = halves(jnp.maximum(enc, 0.0))
-            out = mm3(sd_hi[...], sd_lo[...], hi, lo)
+            hi = jnp.maximum(enc.astype(BF16), jnp.zeros((), BF16))
+            out = mm(sd[...], hi)
             for i in range(2):
                 act[d + i] = hi[2 * C : (2 + B) * C, i * N : (i + 1) * N]
                 pb[d + i + 1] = out[:, i * N : (i + 1) * N]
             return carry
 
-        lax.fori_loop(0, n3 // 2, encode, 0)
+        for i in range(n3 // 2):
+            encode(i, 0)
 
         s2, n2 = span(2)
         sea = lr[edge_rows, :].astype(F32)
@@ -326,27 +359,27 @@
             parts = list(shifts(mis))
             if KM > 3 * E:
                 parts.append(jnp.zeros((KM - 3 * E, N), F32))
-            hi, lo = halves(jnp.concatenate(parts, axis=0))
             at = pl.ds(pl.multiple_of((d + 1) * KM, 16), KM)
-            ms_hi[at, :] = hi
-            ms_lo[at, :] = lo
+            ms[at, :] = jnp.concatenate(parts, axis=0).astype(BF16)
             return carry
 
-        lax.fori_loop(0, n2, misfit, 0)
+        for i in range(n2):
+            misfit(i, 0)
 
         s1, n1 = span(1)
 
         def backward(p, carry):
             d = s1 + 2 * p
-            lifted = mm3(td_hi[...], td_lo[...], pair(ms_hi, d, KM, WM), pair(ms_lo, d, KM, WM))
-            on = jnp.concatenate([act[d], act[d + 1]], axis=1).astype(F32)
-            hi, lo = halves(jnp.where(on > 0.0, lifted, 0.0))
-            out = mm3(se_hi[...], se_lo[...], hi, lo)
+            lifted = mm(td[...], pair(ms, d, KM, WM)).astype(BF16)
+            on = jnp.concatenate([act[d], act[d + 1]], axis=1)
+            zero = jnp.zeros((), BF16)
+            out = mm(se[...], jnp.where(on > zero, lifted, zero))
             for i in range(2):
                 qb[d + i + 1] = out[:, i * N : (i + 1) * N]
             return carry
 
-        lax.fori_loop(0, n1 // 2, backward, 0)
+        for i in range(n1 // 2):
+            backward(i, 0)
 
         ones = (iota((KG - 3 * E, N), 0) < 3).astype(F32)
 
@@ -361,7 +394,8 @@
             g3[pl.ds(pl.multiple_of(i * KG, 16), KG), :] = v.astype(BF16)
             return carry
 
-        lax.fori_loop(0, D, collect, 0)
+        for i in range(D):
+            collect(i, 0)
 
     def sig(v):
         return 0.5 * jnp.tanh(v) + 0.5
@@ -376,7 +410,7 @@
         v = jnp.concatenate(list(shifts(h)), axis=0).astype(BF16)
         h3[pl.ds(pl.multiple_of((d * (L + 2) + lon) * 3 * S, 16), 3 * S), :] = v
 
-    for copy in others:
+    for copy in tiles + others:
         copy.wait()
     x_wait(0, x_ref, 0, 0, 0)
     gradient(0)
@@ -402,19 +436,10 @@
                         hs[side, d] = h.astype(BF16)
         return carry
 
-    lax.fori_loop(0, L, first_gates, 0)
+    lax.fori_loop(0, L, first_gates, 0, unroll=4)
     x_start(1, xr.at[1], o, SLOT, 14)
     for copy in h_copies():
         copy.start()
-
-    for base in range(0, WS, 128):
-        src = iota((9 * ins, 128), 0)
-        lane = iota((9 * ins, 128), 1) + base
-        want = lane + 1
-        for i in range(1, 9):
-            want = want + (lane >= i * S).astype(jnp.int32)
-        pick = ((src == want) & (lane < 9 * S)).astype(F32).astype(BF16)
-        wst[:, base : base + 128] = mm(wide.astype(BF16), pick).astype(BF16)
 
     def state_part(j):
         for p in range(HALF):
@@ -431,7 +456,7 @@
         state_part(j)
         return carry
 
-    lax.fori_loop(1, L - 1, inner, 0)
+    lax.fori_loop(1, L - 1, inner, 0, unroll=2)
     for copy in h_copies():
         copy.wait()
     for d in range(D):
@@ -458,7 +483,7 @@
                 )
         return carry
 
-    lax.fori_loop(0, L, last_gates, 0)
+    lax.fori_loop(0, L, last_gates, 0, unroll=4)
 
 
 def body(n_t, n_l, x, y, m, land, ew, eb, dw, db, gw, gb, ow):
@@ -475,30 +500,31 @@
     scratch = [
         vm((2, W, R, N), F32), vm((D, R, N), F32), vm((D, R, N), jnp.int32), vm((R, N), jnp.int32),
         vm(((W + 2) * KX + WX - 3 * KX, N), BF16), vm(((W + 2) * KX + WX - 3 * KX, N), BF16),
-        vm(((W + 2) * KM + WM - 3 * KM, N), BF16), vm(((W + 2) * KM + WM - 3 * KM, N), BF16),
+        vm(((W + 2) * KM + WM - 3 * KM, N), BF16),
         vm((W, B * C, N), BF16), vm((W + 2, 9 * E, N), F32), vm((W + 2, 9 * E, N), F32),
         vm((W, E, N), F32), vm((D * KG + WG - KG, N), BF16),
         vm((D * (L + 2) * 3 * S + WS - 9 * S, N), BF16),
         vm((2, D, S, N), BF16), vm((2, D, S, N), BF16), vm((L, D // 2, S, 2 * N), F32),
-        vm((E * C, WX), BF16), vm((E * C, WX), BF16), vm((B * C, WM), BF16), vm((B * C, WM), BF16),
-        vm((9 * E, B * C), BF16), vm((9 * E, B * C), BF16),
-        vm((9 * E, E * C), BF16), vm((9 * E, E * C), BF16),
+        vm((E * C, WX), BF16), vm((E * C, WX), BF16), vm((B * C, WM), BF16),
+        vm((9 * E, B * C), BF16), vm((9 * E, E * C), BF16),
         vm((L, G, WG), BF16), vm((G, WS), BF16), vm((L, D // 2, G, 2 * N), F32),
-        pltpu.SemaphoreType.DMA((24,)), pltpu.SemaphoreType.DMA((24,)),
+        pltpu.SemaphoreType.DMA((24,)), pltpu.SemaphoreType.DMA((24,)), pltpu.SemaphoreType.DMA((11,)),
     ]
     v = pl.BlockSpec(memory_space=pltpu.VMEM)
-    specs = [v] * 7 + [pl.BlockSpec(memory_space=pltpu.SMEM)] + [v] * 3
+    whole = pl.BlockSpec(memory_space=pltpu.HBM)
+    weights = (ew, eb[None], dw, db, gw, gb[None], ow[None])
+    scratch = [(pltpu.SMEM if w is db else vm)(w.shape, w.dtype) for w in weights] + scratch
     out = pl.pallas_call(
         functools.partial(kernel, n_t, n_l, D, L, C, S),
         out_shape=jax.ShapeDtypeStruct((D, L, N), F32),
-        in_specs=specs,
+        in_specs=[whole] * 11,
         out_specs=v,
         scratch_shapes=scratch,
         compiler_params=pltpu.CompilerParams(
-            collective_id=0, has_side_effects=True, vmem_limit_bytes=48 << 20
+            collective_id=0, has_side_effects=True, vmem_limit_bytes=67040000
         ),
         name="solver",
-    )(x[0], y[0], m[0], land, ew, eb[None], dw, db, gw, gb[None], ow[None])
+    )(x[0], y[0], m[0], land, *weights)
     return out[None]
 
 

time: 46.1 us -> 32.7 us (0.71)
  Pallas kernels: 38.9 us -> 30.5 us
  local copies, waits for them, and re-layouts: 5.8 us -> 1.32 us
    pallas_call x1, Pallas kernels: 38.9 us -> 30.5 us  [body(): pl.pallas_call(functools.partial(kernel, n_t, n_l, D, L, C, S), out_shape...]
    unnamed x21 -> x1, local copies, waits for them, and re-layouts: 5.8 us -> 1.32 us
where the time goes in v1:
time: 32.7 us; the launch traced here: 32.5 us
  Pallas kernels  30.5 us (93%)
  local copies, waits for them, and re-layouts  1.32 us (4%)
  between operations  0.66 us (2%)
    pallas_call x1, Pallas kernels, body(): pl.pallas_call(functools.partial(kernel, n_t, n_l, D, L, C, S), out_shape...  30.5 us
    unnamed x1, local copies, waits for them, and re-layouts  1.32 us

profile of v1, /device:TPU:0, one launch (start us, length us, event | category | flops | bytes accessed | tf_op | source)
XLA Modules:
  0.0 32.5 jit_solution(17412332386705545860)
XLA Ops:
  0.7 30.5 %solver.1 = f32[4,8,128]{2,1,0:T(8,128)} custom-call(f32[4,8,128]{2,1,0:T(8,128)} %bitcast.8, f32[4,8,128]{2,1,0:T(8,128)} %bitcast.9, s32[4,8,128]{2,1,0:T(8,128)} %bitcast.10, s32[8,128]{1,0:T(8,128)} %land_ref.1, f32[32,27]{1,0:T(8,128)} %rest_0_.1, f32[1,32]{1,0:T(1,128)} %bitcast.12, f32[32,27]{1,0:T(8,128)} %rest_2_.1, f32[1]{0:T(128)S(6)} %copy.13.rest_3_, ...), custom_call_target="tpu_custom_call" | custom-call | tf_op jit(solution)/shard_map/solver/pallas_call | solution.py:517
  31.2 1.3 %copy.14 = f32[1,4,8,128]{3,2,1,0:T(8,128)} copy(f32[1,4,8,128]{3,2,1,0:T(8,128)} %bitcast.7) | data formatting | bytes 32768
